TPU v7x, 128 devices: a whole 4x4x4 slice. The times are simulated.
128 devices in a mesh: cells: 64 (over y, z, x), members: 2 (over core).
Axes of the slice: x: 4, y: 4, z: 4, core: 2. Of those that a mesh axis runs over, the one named last changes fastest.
Arguments:
- ensemble: float32 [64, 4, 65536], P('members', None, 'cells')
- speed: float32 [65536], P('cells'), may hold values from 0.1 to 0.85
- direction: int32 [65536], P('cells'), may hold values 0 or 1
- couple: float32 [4, 4], replicated, may hold values from -0.25 to 0.25
- obs_place: int32 [16384], P('cells'), may hold values from 0 to 1023
- obs_field: int32 [16384], P('cells'), may hold values from 0 to 3
- obs_value: float32 [16384], P('cells'), may hold values from -8 to 8
- obs_sigma: float32 [16384], P('cells'), may hold values from 0.5 to 5
- send_count: int32 [64, 64], P('cells'), may hold values from 0 to 32, as said below
Outputs:
- analysis: float32 [64, 4, 65536], P('members', None, 'cells')
- innovation: float32 [16384], P('cells')
Inputs may be any that keep to these rules, and one draw needn't show every extreme that they name: Each row of send_count sums to 256; no entry exceeds 32; in every row four blocks get exactly 32, and one block gets exactly 32 from every row.
All inputs are finite; a program needn't handle non-finite values. No bound on the sum of `direction` on one device may be relied on, other than what follows from the above.
Results may differ from a plain program's by a relative error of at most 0.0001.
Values sent between devices are 32-bit elements; how exact they have to be, the bound alone decides.
A program may use at most 64 MiB of HBM per device.

v0:
```python
import math
import jax
import jax.numpy as jnp
from jax import lax
from jax.sharding import PartitionSpec as P

STEPS = 4
OBS_DEV = 256
CAP = 32
DIFFUSION = 0.05


def padded_2(cells, sides, width):
    for axis, dim in sides:
        count = lax.axis_size(axis)
        ends = count - 1
        head = lax.slice_in_dim(cells, 0, width, axis=dim)
        tail = lax.slice_in_dim(cells, cells.shape[dim] - width, cells.shape[dim], axis=dim)
        cells = jnp.concatenate(
            [
                lax.ppermute(tail, axis, [(i, (i + 1) % count) for i in range(ends)]),
                cells,
                lax.ppermute(head, axis, [((i + 1) % count, i) for i in range(ends)]),
            ],
            axis=dim,
        )
    return cells


def factor_lower(matrix):
    order = matrix.shape[0]
    row_ids = jnp.arange(order, dtype=jnp.int32)

    def column_step(col, lower):
        column = lax.dynamic_slice_in_dim(matrix, col, 1, 1)[:, 0]
        done_row = lax.dynamic_slice_in_dim(lower, col, 1, 0)[0]
        reduced = column - jnp.dot(lower, done_row, precision=lax.Precision.HIGHEST)
        pivot = jnp.sqrt(lax.dynamic_slice_in_dim(reduced, col, 1, 0)[0])
        values = jnp.where(row_ids >= col, reduced / pivot, 0.0)
        return lax.dynamic_update_slice_in_dim(lower, values[:, None], col, 1)

    return lax.fori_loop(0, order, column_step, jnp.zeros_like(matrix))


def invert_lower(lower):
    order = lower.shape[0]
    identity = jnp.eye(order, dtype=jnp.float32)
    diagonal_values = jnp.diagonal(lower)
    nilpotent = identity - lower / diagonal_values[:, None]
    result = identity + nilpotent
    power = nilpotent
    for level in range(max(order - 1, 1).bit_length() - 1):
        power = jnp.dot(power, power, precision=lax.Precision.HIGHEST)
        result = jnp.dot(result, identity + power, precision=lax.Precision.HIGHEST)
    return result / diagonal_values[None, :]


def mixing_matrix(upper_factor, carried, members):
    upper_inverse = invert_lower(upper_factor.T).T
    mean_weights = jnp.dot(upper_inverse, carried, precision=lax.Precision.HIGHEST)
    identity = jnp.eye(members, dtype=jnp.float32)
    spread = math.sqrt(members - 1.0) * upper_inverse
    centering = identity - 1.0 / members
    shifted = jnp.dot(centering, mean_weights, precision=lax.Precision.HIGHEST)
    inner = jnp.dot(
        jnp.dot(centering, spread, precision=lax.Precision.HIGHEST),
        centering,
        precision=lax.Precision.HIGHEST,
    )
    return 1.0 / members + shifted[:, None] + inner


def couple_fields(couple, advanced):
    return advanced + jnp.einsum("fg,kgc->kfc", couple, advanced, precision=lax.Precision.HIGHEST)


def shards(
    ensemble, speed, direction, couple, obs_place, obs_field, obs_value, obs_sigma, send_count
):
    local_members, fields, cells_here = ensemble.shape
    owners = lax.axis_size("cells")
    members = local_members * lax.axis_size("members")
    flag_values = direction.astype(jnp.float32)
    toward_left = speed * flag_values
    toward_right = speed - toward_left
    states = ensemble
    for step_index in range(STEPS):
        padded = padded_2(states, (("cells", 2),), 1)
        left_cells = padded[:, :, :-2]
        right_cells = padded[:, :, 2:]
        advanced = (
            states
            + toward_left * left_cells
            + toward_right * right_cells
            - speed * states
            + DIFFUSION * (left_cells - 2.0 * states + right_cells)
        )
        states = couple_fields(couple, advanced)
    counts_row = send_count[0]
    owner_ends = jnp.cumsum(counts_row)
    starts = owner_ends - counts_row
    slot_ids = jnp.arange(OBS_DEV, dtype=jnp.int32)
    owner_of = jnp.sum((owner_ends[None, :] <= slot_ids[:, None]).astype(jnp.int32), axis=1)
    owner_match = owner_of[:, None] == jnp.arange(owners, dtype=jnp.int32)[None, :]
    start_of = jnp.sum(jnp.where(owner_match, starts[None, :], 0), axis=1)
    position = owner_of * CAP + slot_ids - start_of
    slot_grid = jnp.arange(CAP, dtype=jnp.int32)
    source_slot = jnp.minimum(starts[:, None] + slot_grid[None, :], OBS_DEV - 1)
    live_slot = slot_grid[None, :] < counts_row[:, None]
    request = jnp.where(live_slot, obs_field[source_slot] * cells_here + obs_place[source_slot], 0)
    flat_states = states.reshape(local_members, fields * cells_here)
    asked_slots = lax.all_to_all(request, "cells", split_axis=0, concat_axis=0, tiled=True)
    found_values = jnp.take(flat_states, asked_slots.reshape(-1), axis=1)
    found_values = found_values.reshape(local_members, asked_slots.shape[0], asked_slots.shape[1])
    returned = lax.all_to_all(found_values, "cells", split_axis=1, concat_axis=1, tiled=True)
    local_values = jnp.take(returned.reshape(local_members, owners * CAP), position, axis=1)
    all_values = lax.all_gather(local_values, "members", axis=0, tiled=True)
    center = jnp.mean(all_values, axis=0)
    scaled_anomaly = (all_values - center) / obs_sigma
    innovation = (obs_value - center) / obs_sigma
    augmented = jnp.concatenate([scaled_anomaly, innovation[None, :]], axis=0)
    local_gram = jnp.dot(augmented, augmented.T, precision=lax.Precision.HIGHEST)
    summed_gram = lax.psum(local_gram, "cells")
    diagonal_add = jnp.concatenate(
        [jnp.full((members,), members - 1.0, jnp.float32), jnp.ones((1,), jnp.float32)]
    )
    factor = factor_lower(summed_gram + jnp.diag(diagonal_add)).T
    mixing = mixing_matrix(factor[:members, :members], factor[:members, members], members)
    member_index = lax.axis_index("members")
    own_rows = lax.dynamic_slice_in_dim(mixing, member_index * local_members, local_members, 0)
    analysis = lax.psum_scatter(
        jnp.einsum("kj,kfc->jfc", own_rows, states, precision=lax.Precision.HIGHEST),
        "members",
        scatter_dimension=0,
        tiled=True,
    )
    return (analysis, innovation)


def solution(mesh):
    return jax.shard_map(
        shards,
        mesh=mesh,
        in_specs=(
            P("members", None, "cells"),
            P("cells"),
            P("cells"),
            P(),
            P("cells"),
            P("cells"),
            P("cells"),
            P("cells"),
            P("cells", None),
        ),
        out_specs=(P("members", None, "cells"), P("cells")),
        check_vma=False,
    )
```

profile of v0, /device:TPU:1, one launch (start us, length us, event | category | flops | bytes accessed | tf_op | source)
XLA Modules:
  0.0 626.4 jit_solution(9575588575575584767)
XLA Ops:
  7.2 1.0 fusion.125
  8.2 3.9 collective-permute-start
  12.1 1.3 collective-permute-start.1
  13.4 0.7 copy.33
  14.4 0.7 bitcast_subtract_fusion.1
  15.2 13.2 %gather_fusion = s32[2048]{0:T(1024)S(1)} fusion(s32[256]{0:T(256)S(1)} %copy-done.1, s32[2048]{0:T(1024)S(1)} %broadcast_clamp_fusion.1), kind=kCustom, calls=%fused_computation | custom fusion | bytes 24576 | tf_op jit(solution)/shard_map/gather | solution.py:110
  28.5 13.2 %gather_fusion.1 = s32[2048]{0:T(1024)S(1)} fusion(s32[256]{0:T(256)S(1)} %copy-done.2, s32[2048]{0:T(1024)S(1)} %broadcast_clamp_fusion.1), kind=kCustom, calls=%fused_computation.1 | custom fusion | bytes 24576 | tf_op jit(solution)/shard_map/gather | solution.py:110
  41.8 0.7 fusion.87
  42.5 12.0 %all-to-all-start = ((s32[64,1,32]{2,1,0:T(1,128)}), s32[64,1,32]{2,1,0:T(1,128)S(1)}, u32[]{:S(2)}, u32[]{:S(2)}) async-start(s32[64,1,32]{2,1,0:T(1,128)} %bitcast.3), calls=%async_computation | async-start | bytes 65536 | tf_op jit(solution)/shard_map/all_to_all | solution.py:112
  54.7 2.2 fusion.10
  57.0 2.9 collective-permute-start.2
  59.9 1.3 collective-permute-start.3
  61.3 3.8 collective-permute-done.3
  65.1 2.2 fusion.9
  67.4 2.9 collective-permute-start.4
  70.3 1.3 collective-permute-start.5
  71.6 3.7 collective-permute-done.5
  75.3 2.2 fusion.8
  77.6 4.6 collective-permute-start.6
  82.3 1.5 collective-permute-start.7
  83.8 3.5 collective-permute-done.7
  87.3 2.2 fusion.7
  89.5 0.6 copy.40
  90.7 0.7 reduce.5
  91.5 7.6 %gather_fusion.2 = f32[2048,32]{1,0:T(8,128)} fusion(f32[32,4096]{0,1:T(8,128)S(1)} %bitcast.118, s32[2048]{0:T(1024)S(1)} %broadcast_clamp_fusion), kind=kCustom, calls=%fused_computation.2 | custom fusion | bytes 532480 | tf_op jit(solution)/shard_map/jit(_take)/gather | solution.py:113
  99.1 1.6 fusion.126
  100.7 1.2 reshape.299
  101.9 18.0 %all-to-all-start.1 = ((f32[64,1,1024]{2,1,0:T(1,128)}), f32[64,1,1024]{2,1,0:T(1,128)S(1)}, u32[]{:S(2)}, u32[]{:S(2)}) async-start(f32[64,1,1024]{2,1,0:T(1,128)} %reshape.299), calls=%async_computation.1 | async-start | bytes 524288 | tf_op jit(solution)/shard_map/all_to_all | solution.py:115
  120.0 9.4 %all-to-all-done.1 = f32[64,1,1024]{2,1,0:T(1,128)S(1)} async-done(((f32[64,1,1024]{2,1,0:T(1,128)}), f32[64,1,1024]{2,1,0:T(1,128)S(1)}, u32[]{:S(2)}, u32[]{:S(2)}) %all-to-all-start.1) | async-done | bytes 262176 | tf_op jit(solution)/shard_map/all_to_all | solution.py:115
  129.9 1.3 reduce.6
  131.5 0.7 gather_fusion.3
  132.4 8.5 %all_gather.3 = f32[64,256]{1,0:T(8,128)S(1)} all-gather(f32[32,256]{1,0:T(8,128)S(1)} %copy.36), channel_id=1, replica_groups=mesh['cells'=64,'members'=2] {'members'}, dimensions={0}, use_global_device_ids=true | all-gather | bytes 98304 | tf_op jit(solution)/shard_map/all_gather | solution.py:117
  141.2 288.0 %psum.7 = f32[65,65]{1,0:T(8,128)S(1)} all-reduce(f32[65,65]{1,0:T(8,128)S(1)} %fusion.76), channel_id=1, replica_groups=mesh['cells'=64,'members'=2] {'cells'}, use_global_device_ids=true, to_apply=%region_4.5 | all-reduce | flops 4225 | bytes 33800 | tf_op jit(solution)/shard_map/psum | solution.py:123
  429.4 120.6 %while.14 = (s32[]{:T(128)}, f32[65,65]{1,0:T(8,128)S(1)}, f32[65,65]{0,1:T(8,128)S(1)}, s32[]{:T(128)}, s32[]{:T(128)}) while((s32[]{:T(128)}, f32[65,65]{1,0:T(8,128)S(1)}, f32[65,65]{0,1:T(8,128)S(1)}, s32[]{:T(128)}, s32[]{:T(128)}) %tuple.49), condition=%wide.region_6.7_spmd.clone, body=%wide.region_5.6_spmd.clone.sunk | while | flops 50962 | bytes 40825 | solution.py:42
  429.6 0.6 dynamic_slice.43
  431.3 0.6 dynamic_slice.43
  435.0 0.6 dynamic_slice.43
  438.8 0.6 dynamic_slice.43
  440.6 0.6 dynamic_slice.43
  442.5 0.6 dynamic_slice.43
  444.3 0.6 dynamic_slice.43
  448.0 0.6 dynamic_slice.43
  451.8 0.6 dynamic_slice.43
  453.6 0.6 dynamic_slice.43
  550.1 0.8 gather_fusion.4
  553.6 3.5 fusion.89
  557.1 60.3 %reduce-scatter.2.cloned.1.call-done = f32[32,4,1024]{2,0,1:T(8,128)} async-done(((f32[64,4,1024]{2,0,1:T(8,128)}), f32[32,4,1024]{2,0,1:T(8,128)}) %reduce-scatter.2.cloned.1.call-update) | async-done | bytes 524304 | tf_op jit(solution)/shard_map/reduce_scatter | solution.py:131
  617.4 2.2 copy.39
  (396 shorter events, 73.2 us)
Async XLA Ops:
  7.2 47.5 %copy-start = (f32[4,4]{1,0:T(4,128)S(1)}, f32[4,4]{1,0:T(4,128)}, u32[]{:S(2)}) copy-start(f32[4,4]{1,0:T(4,128)} %param.14) | copy-start | bytes 196
  7.2 8.0 %copy-start.1 = (s32[256]{0:T(256)S(1)}, s32[256]{0:T(256)}, u32[]{:S(2)}) copy-start(s32[256]{0:T(256)} %param.16) | copy-start | bytes 3076
  8.2 46.5 %collective-permute-start = (f32[32,4,1]{2,1,0:T(4,128)S(1)}, f32[32,4,1]{2,1,0:T(4,128)S(1)}, u32[]{:S(2)}, u32[]{:S(2)}) collective-permute-start(f32[32,4,1]{2,1,0:T(4,128)S(1)} %get-tuple-element.122), channel_id=1, source_target_pairs={{0,2},{2,4},{4,6},{6,8},{8,10},{10,12},{12,14},{14,16},{16,18},{18... | collective-permute-start | bytes 1544 | tf_op jit(solution)/shard_map/ppermute | solution.py:21
  12.1 42.5 %collective-permute-start.1 = (f32[32,4,1]{2,1,0:T(4,128)S(1)}, f32[32,4,1]{2,1,0:T(4,128)S(1)}, u32[]{:S(2)}, u32[]{:S(2)}) collective-permute-start(f32[32,4,1]{2,1,0:T(4,128)S(1)} %get-tuple-element.123), channel_id=1, source_target_pairs={{2,0},{4,2},{6,4},{8,6},{10,8},{12,10},{14,12},{16,14},{18,16},{20... | collective-permute-start | bytes 1544 | tf_op jit(solution)/shard_map/ppermute | solution.py:23
  15.2 13.2 %copy-start.2 = (s32[256]{0:T(256)S(1)}, s32[256]{0:T(256)}, u32[]{:S(2)}) copy-start(s32[256]{0:T(256)} %param.15) | copy-start | bytes 3076
  28.4 13.3 %copy-start.8 = (s32[1,64]{1,0:T(1,128)S(1)}, s32[1,64]{1,0:T(1,128)}, u32[]{:S(2)}) copy-start(s32[1,64]{1,0:T(1,128)} %param.19) | copy-start | bytes 772
  28.4 26.1 %copy-start.6 = (s32[1024]{0:T(1024)S(1)}, s32[1024]{0:T(1024)}, u32[]{:S(2)}) copy-start(s32[1024]{0:T(1024)} %param.13) | copy-start | bytes 12292
  28.5 26.1 %copy-start.7 = (f32[1024]{0:T(1024)S(1)}, f32[1024]{0:T(1024)}, u32[]{:S(2)}) copy-start(f32[1024]{0:T(1024)} %param.12) | copy-start | bytes 12292
  28.5 26.2 %copy-start.3 = (f32[32,4,1024]{2,1,0:T(4,128)S(1)}, f32[32,4,1024]{2,1,0:T(4,128)}, u32[]{:S(2)}) copy-start(f32[32,4,1024]{2,1,0:T(4,128)} %param.11) | copy-start | bytes 1572868
  42.5 47.7 %all-to-all-start = ((s32[64,1,32]{2,1,0:T(1,128)}), s32[64,1,32]{2,1,0:T(1,128)S(1)}, u32[]{:S(2)}, u32[]{:S(2)}) async-start(s32[64,1,32]{2,1,0:T(1,128)} %bitcast.3), calls=%async_computation | async-start | bytes 65536 | tf_op jit(solution)/shard_map/all_to_all | solution.py:112
  57.0 4.3 collective-permute-start.2
  59.9 5.2 collective-permute-start.3
  67.4 4.2 collective-permute-start.4
  70.3 5.0 collective-permute-start.5
  77.6 6.1 collective-permute-start.6
  82.3 5.0 collective-permute-start.7
  100.7 40.2 %copy-start.4 = (f32[256]{0:T(256)S(1)}, f32[256]{0:T(256)}, u32[]{:S(2)}) copy-start(f32[256]{0:T(256)} %param.18) | copy-start | bytes 3076
  100.7 40.2 %copy-start.9 = (f32[256]{0:T(256)S(1)}, f32[256]{0:T(256)}, u32[]{:S(2)}) copy-start(f32[256]{0:T(256)} %param.17) | copy-start | bytes 3076
  101.9 327.3 %copy-start.10 = (f32[65]{0:T(128)S(1)}, f32[65]{0:T(128)}, u32[]{:S(2)}) copy-start(f32[65]{0:T(128)} %constant.99.clone.1) | copy-start | bytes 784
  101.9 27.5 %all-to-all-start.1 = ((f32[64,1,1024]{2,1,0:T(1,128)}), f32[64,1,1024]{2,1,0:T(1,128)S(1)}, u32[]{:S(2)}, u32[]{:S(2)}) async-start(f32[64,1,1024]{2,1,0:T(1,128)} %reshape.299), calls=%async_computation.1 | async-start | bytes 524288 | tf_op jit(solution)/shard_map/all_to_all | solution.py:115
  119.9 497.5 %reduce-scatter.2.cloned.1.call-start = ((), (), s32[]{:S(2)}) async-start(), calls=%async_computation.3 | async-start | bytes 1572864 | tf_op jit(solution)/shard_map/reduce_scatter | solution.py:131
  140.9 416.1 %copy-start.5 = (f32[256]{0:T(256)}, f32[256]{0:T(256)S(1)}, u32[]{:S(2)}) copy-start(f32[256]{0:T(256)S(1)} %get-tuple-element.127) | copy-start | bytes 3076
Sparse Core Ops, SparseCore 0:
  557.2 60.1 reduce-scatter.1
where the time goes:
time: 632 us; the launch traced here: 626 us
  blocking collectives  297 us (47%)
  local copies, waits for them, and re-layouts  107 us (17%)
  waiting for transfers between devices  80.7 us (13%)
  starting transfers between devices  49.8 us (8%)
  loops' own time  47.1 us (7%)
  matrix products  24.6 us (4%)
  between operations  14.6 us (2%)
    psum x1, blocking collectives, shards(): summed_gram = lax.psum(local_gram, 'cells')  288 us
    reduce_scatter x1, waiting for transfers between devices, shards(): lax.psum_scatter(jnp.einsum('kj,kfc->jfc', own_rows, states, precision=la...  60.3 us
    another operation x1, loops' own time, factor_lower(): return lax.fori_loop(0, order, column_step, jnp.zeros_like(matrix))  47.1 us
    dynamic_slice x65, local copies, waits for them, and re-layouts, column_step(): pivot = jnp.sqrt(lax.dynamic_slice_in_dim(reduced, col, 1, 0)[0])  40.3 us
    all_to_all x1, starting transfers between devices, shards(): lax.all_to_all(found_values, 'cells', split_axis=1, concat_axis=1, tiled=...  18 us
    dynamic_update_slice x65, local copies, waits for them, and re-layouts, column_step(): return lax.dynamic_update_slice_in_dim(lower, values[:, None], col, 1)  16.2 us
    ppermute x4, starting transfers between devices, padded_2(): lax.ppermute(tail, axis, [(i, (i + 1) % count) for i in range(ends)])  14.4 us
    gather x1, local copies, waits for them, and re-layouts, shards(): obs_field[source_slot] * cells_here + obs_place[source_slot]  13.2 us
  transfers between devices with their start and end apart: 11, of which 5 were waited for; matrix products, arithmetic and copies ran while one was open for 6% of the time, Pallas kernels for 0%

commit v1 on v0

--- a/solution.py
+++ b/solution.py
@@ -120,7 +120,8 @@
     innovation = (obs_value - center) / obs_sigma
     augmented = jnp.concatenate([scaled_anomaly, innovation[None, :]], axis=0)
     local_gram = jnp.dot(augmented, augmented.T, precision=lax.Precision.HIGHEST)
-    summed_gram = lax.psum(local_gram, "cells")
+    arr_out = lax.all_gather(local_gram, "cells")
+    summed_gram = jnp.sum(arr_out, axis=0)
     diagonal_add = jnp.concatenate(
         [jnp.full((members,), members - 1.0, jnp.float32), jnp.ones((1,), jnp.float32)]
     )

time: 632 us -> 356 us (0.56)
  blocking collectives: 297 us -> 8.45 us
  waiting for transfers between devices: 80.7 us -> 90.9 us
    psum x1 -> x0, blocking collectives: 288 us -> none  [shards(): summed_gram = lax.psum(local_gram, 'cells')]
    all_gather x0 -> x1, waiting for transfers between devices: none -> 60.2 us  [shards(): arr_out = lax.all_gather(local_gram, 'cells')]
    reduce_scatter x1, waiting for transfers between devices: 60.3 us -> 10.3 us  [shards(): lax.psum_scatter(jnp.einsum('kj,kfc->jfc', own_rows, states, precision=la...]
  transfers between devices with their start and end apart: 11 -> 12, of which waited for: 5 -> 6; matrix products, arithmetic and copies ran while one was open for 6% -> 11% of each run, Pallas kernels for 0% -> 0%
where the time goes in v1:
time: 356 us; the launch traced here: 351 us
  local copies, waits for them, and re-layouts  107 us (30%)
  waiting for transfers between devices  90.9 us (26%)
  starting transfers between devices  49.7 us (14%)
  loops' own time  47.1 us (13%)
  matrix products  25.1 us (7%)
  between operations  14.6 us (4%)
  blocking collectives  8.45 us (2%)
  other arithmetic  7.93 us (2%)
    all_gather x1, waiting for transfers between devices, shards(): arr_out = lax.all_gather(local_gram, 'cells')  60.2 us
    another operation x1, loops' own time, factor_lower(): return lax.fori_loop(0, order, column_step, jnp.zeros_like(matrix))  47.1 us
    dynamic_slice x65, local copies, waits for them, and re-layouts, column_step(): pivot = jnp.sqrt(lax.dynamic_slice_in_dim(reduced, col, 1, 0)[0])  40.3 us
    all_to_all x1, starting transfers between devices, shards(): lax.all_to_all(found_values, 'cells', split_axis=1, concat_axis=1, tiled=...  17.9 us
    dynamic_update_slice x65, local copies, waits for them, and re-layouts, column_step(): return lax.dynamic_update_slice_in_dim(lower, values[:, None], col, 1)  16.2 us
    ppermute x4, starting transfers between devices, padded_2(): lax.ppermute(tail, axis, [(i, (i + 1) % count) for i in range(ends)])  14.4 us
    gather x1, local copies, waits for them, and re-layouts, shards(): obs_field[source_slot] * cells_here + obs_place[source_slot]  13.2 us
    gather x1, local copies, waits for them, and re-layouts, shards(): obs_place[source_slot]  13.2 us
  transfers between devices with their start and end apart: 12, of which 6 were waited for; matrix products, arithmetic and copies ran while one was open for 11% of the time, Pallas kernels for 0%

profile of v1, /device:TPU:1, one launch (start us, length us, event | category | flops | bytes accessed | tf_op | source)
XLA Modules:
  0.0 350.9 jit_solution(2498511892987684119)
XLA Ops:
  7.2 1.0 fusion.124
  8.2 3.9 %collective-permute-start = (f32[32,4,1]{2,1,0:T(4,128)S(1)}, f32[32,4,1]{2,1,0:T(4,128)S(1)}, u32[]{:S(2)}, u32[]{:S(2)}) collective-permute-start(f32[32,4,1]{2,1,0:T(4,128)S(1)} %get-tuple-element.116), channel_id=1, source_target_pairs={{0,2},{2,4},{4,6},{6,8},{8,10},{10,12},{12,14},{14,16},{16,18},{18... | collective-permute-start | bytes 1544 | tf_op jit(solution)/shard_map/ppermute | solution.py:21
  12.1 1.3 collective-permute-start.1
  13.4 0.7 copy.33
  14.4 0.7 bitcast_subtract_fusion.1
  15.2 13.2 %gather_fusion = s32[2048]{0:T(1024)S(1)} fusion(s32[256]{0:T(256)S(1)} %copy-done.1, s32[2048]{0:T(1024)S(1)} %broadcast_clamp_fusion.1), kind=kCustom, calls=%fused_computation | custom fusion | bytes 24576 | tf_op jit(solution)/shard_map/gather | solution.py:110
  28.5 13.2 %gather_fusion.1 = s32[2048]{0:T(1024)S(1)} fusion(s32[256]{0:T(256)S(1)} %copy-done.2, s32[2048]{0:T(1024)S(1)} %broadcast_clamp_fusion.1), kind=kCustom, calls=%fused_computation.1 | custom fusion | bytes 24576 | tf_op jit(solution)/shard_map/gather | solution.py:110
  41.8 0.7 fusion.86
  42.5 12.0 %all-to-all-start = ((s32[64,1,32]{2,1,0:T(1,128)}), s32[64,1,32]{2,1,0:T(1,128)S(1)}, u32[]{:S(2)}, u32[]{:S(2)}) async-start(s32[64,1,32]{2,1,0:T(1,128)} %bitcast.3), calls=%async_computation | async-start | bytes 65536 | tf_op jit(solution)/shard_map/all_to_all | solution.py:112
  54.7 2.2 fusion.10
  56.9 2.9 collective-permute-start.2
  59.9 1.3 collective-permute-start.3
  61.2 3.9 %collective-permute-done.3 = f32[32,4,1]{2,1,0:T(4,128)S(1)} collective-permute-done((f32[32,4,1]{2,1,0:T(4,128)S(1)}, f32[32,4,1]{2,1,0:T(4,128)S(1)}, u32[]{:S(2)}, u32[]{:S(2)}) %collective-permute-start.3) | collective-permute-done | bytes 544 | tf_op jit(solution)/shard_map/ppermute | solution.py:23
  65.1 2.2 fusion.9
  67.4 2.9 collective-permute-start.4
  70.3 1.3 collective-permute-start.5
  71.7 3.6 %collective-permute-done.5 = f32[32,4,1]{2,1,0:T(4,128)S(1)} collective-permute-done((f32[32,4,1]{2,1,0:T(4,128)S(1)}, f32[32,4,1]{2,1,0:T(4,128)S(1)}, u32[]{:S(2)}, u32[]{:S(2)}) %collective-permute-start.5) | collective-permute-done | bytes 544 | tf_op jit(solution)/shard_map/ppermute | solution.py:23
  75.3 2.2 fusion.8
  77.6 4.6 %collective-permute-start.6 = (f32[32,4,1]{2,1,0:T(4,128)S(1)}, f32[32,4,1]{2,1,0:T(4,128)S(1)}, u32[]{:S(2)}, u32[]{:S(2)}) collective-permute-start(f32[32,4,1]{2,1,0:T(4,128)S(1)} %get-tuple-element.110), channel_id=1, source_target_pairs={{0,2},{2,4},{4,6},{6,8},{8,10},{10,12},{12,14},{14,16},{16,18},{18... | collective-permute-start | bytes 1544 | tf_op jit(solution)/shard_map/ppermute | solution.py:21
  82.2 1.5 collective-permute-start.7
  83.7 3.5 collective-permute-done.7
  87.2 2.2 fusion.7
  89.4 0.6 copy.40
  90.6 0.7 reduce.6
  91.5 7.6 %gather_fusion.2 = f32[2048,32]{1,0:T(8,128)} fusion(f32[32,4096]{0,1:T(8,128)S(1)} %bitcast.120, s32[2048]{0:T(1024)S(1)} %broadcast_clamp_fusion), kind=kCustom, calls=%fused_computation.2 | custom fusion | bytes 532480 | tf_op jit(solution)/shard_map/jit(_take)/gather | solution.py:113
  99.1 1.6 fusion.125
  100.7 1.2 reshape.303
  101.8 17.9 %all-to-all-start.1 = ((f32[64,1,1024]{2,1,0:T(1,128)}), f32[64,1,1024]{2,1,0:T(1,128)S(1)}, u32[]{:S(2)}, u32[]{:S(2)}) async-start(f32[64,1,1024]{2,1,0:T(1,128)} %reshape.303), calls=%async_computation.1 | async-start | bytes 524288 | tf_op jit(solution)/shard_map/all_to_all | solution.py:115
  119.8 9.4 %all-to-all-done.1 = f32[64,1,1024]{2,1,0:T(1,128)S(1)} async-done(((f32[64,1,1024]{2,1,0:T(1,128)}), f32[64,1,1024]{2,1,0:T(1,128)S(1)}, u32[]{:S(2)}, u32[]{:S(2)}) %all-to-all-start.1) | async-done | bytes 262176 | tf_op jit(solution)/shard_map/all_to_all | solution.py:115
  129.7 1.3 reduce.7
  131.3 0.7 gather_fusion.3
  132.2 8.5 %all_gather.9 = f32[64,256]{1,0:T(8,128)S(1)} all-gather(f32[32,256]{1,0:T(8,128)S(1)} %copy.36), channel_id=1, replica_groups=mesh['cells'=64,'members'=2] {'members'}, dimensions={0}, use_global_device_ids=true | all-gather | bytes 98304 | tf_op jit(solution)/shard_map/all_gather | solution.py:117
  140.8 0.8 convolution_bitcast_fusion.5
  141.7 60.2 %all-gather.4.cloned.1.call-done = f32[64,65,65]{2,1,0:T(8,128)} async-done(((f32[1,65,65]{2,1,0:T(8,128)}), f32[64,65,65]{2,1,0:T(8,128)}) %all-gather.4.cloned.1.call-update) | async-done | bytes 1081616 | tf_op jit(solution)/shard_map/all_gather | solution.py:123
  201.9 1.9 reduce_sum.42
  203.9 120.6 %while.14 = (s32[]{:T(128)}, f32[65,65]{1,0:T(8,128)S(1)}, f32[65,65]{0,1:T(8,128)S(1)}, s32[]{:T(128)}, s32[]{:T(128)}) while((s32[]{:T(128)}, f32[65,65]{1,0:T(8,128)S(1)}, f32[65,65]{0,1:T(8,128)S(1)}, s32[]{:T(128)}, s32[]{:T(128)}) %tuple.47), condition=%wide.region_6.7_spmd.clone, body=%wide.region_5.6_spmd.clone.sunk | while | flops 50962 | bytes 40825 | solution.py:42
  204.1 0.6 dynamic_slice.43
  207.7 0.6 dynamic_slice.43
  211.4 0.6 dynamic_slice.43
  213.3 0.6 dynamic_slice.43
  217.0 0.6 dynamic_slice.43
  220.7 0.6 dynamic_slice.43
  222.6 0.6 dynamic_slice.43
  224.4 0.6 dynamic_slice.43
  324.6 0.8 gather_fusion.4
  328.1 3.5 fusion.88
  331.6 10.3 %reduce-scatter.2.cloned.1.call-done = f32[32,4,1024]{2,0,1:T(8,128)} async-done(((f32[64,4,1024]{2,0,1:T(8,128)}), f32[32,4,1024]{2,0,1:T(8,128)}) %reduce-scatter.2.cloned.1.call-update) | async-done | bytes 524304 | tf_op jit(solution)/shard_map/reduce_scatter | solution.py:132
  341.9 2.2 copy.39
  (399 shorter events, 74.3 us)
Async XLA Ops:
  7.2 47.5 %copy-start = (f32[4,4]{1,0:T(4,128)S(1)}, f32[4,4]{1,0:T(4,128)}, u32[]{:S(2)}) copy-start(f32[4,4]{1,0:T(4,128)} %param.14) | copy-start | bytes 196
  7.2 8.0 %copy-start.1 = (s32[256]{0:T(256)S(1)}, s32[256]{0:T(256)}, u32[]{:S(2)}) copy-start(s32[256]{0:T(256)} %param.16) | copy-start | bytes 3076
  8.2 46.4 %collective-permute-start = (f32[32,4,1]{2,1,0:T(4,128)S(1)}, f32[32,4,1]{2,1,0:T(4,128)S(1)}, u32[]{:S(2)}, u32[]{:S(2)}) collective-permute-start(f32[32,4,1]{2,1,0:T(4,128)S(1)} %get-tuple-element.116), channel_id=1, source_target_pairs={{0,2},{2,4},{4,6},{6,8},{8,10},{10,12},{12,14},{14,16},{16,18},{18... | collective-permute-start | bytes 1544 | tf_op jit(solution)/shard_map/ppermute | solution.py:21
  12.1 42.5 %collective-permute-start.1 = (f32[32,4,1]{2,1,0:T(4,128)S(1)}, f32[32,4,1]{2,1,0:T(4,128)S(1)}, u32[]{:S(2)}, u32[]{:S(2)}) collective-permute-start(f32[32,4,1]{2,1,0:T(4,128)S(1)} %get-tuple-element.117), channel_id=1, source_target_pairs={{2,0},{4,2},{6,4},{8,6},{10,8},{12,10},{14,12},{16,14},{18,16},{20... | collective-permute-start | bytes 1544 | tf_op jit(solution)/shard_map/ppermute | solution.py:23
  15.2 13.2 %copy-start.2 = (s32[256]{0:T(256)S(1)}, s32[256]{0:T(256)}, u32[]{:S(2)}) copy-start(s32[256]{0:T(256)} %param.15) | copy-start | bytes 3076
  28.4 13.3 %copy-start.8 = (s32[1,64]{1,0:T(1,128)S(1)}, s32[1,64]{1,0:T(1,128)}, u32[]{:S(2)}) copy-start(s32[1,64]{1,0:T(1,128)} %param.19) | copy-start | bytes 772
  28.4 26.1 %copy-start.6 = (s32[1024]{0:T(1024)S(1)}, s32[1024]{0:T(1024)}, u32[]{:S(2)}) copy-start(s32[1024]{0:T(1024)} %param.13) | copy-start | bytes 12292
  28.5 26.1 %copy-start.7 = (f32[1024]{0:T(1024)S(1)}, f32[1024]{0:T(1024)}, u32[]{:S(2)}) copy-start(f32[1024]{0:T(1024)} %param.12) | copy-start | bytes 12292
  28.5 26.2 %copy-start.3 = (f32[32,4,1024]{2,1,0:T(4,128)S(1)}, f32[32,4,1024]{2,1,0:T(4,128)}, u32[]{:S(2)}) copy-start(f32[32,4,1024]{2,1,0:T(4,128)} %param.11) | copy-start | bytes 1572868
  42.5 47.6 %all-to-all-start = ((s32[64,1,32]{2,1,0:T(1,128)}), s32[64,1,32]{2,1,0:T(1,128)S(1)}, u32[]{:S(2)}, u32[]{:S(2)}) async-start(s32[64,1,32]{2,1,0:T(1,128)} %bitcast.3), calls=%async_computation | async-start | bytes 65536 | tf_op jit(solution)/shard_map/all_to_all | solution.py:112
  56.9 4.2 %collective-permute-start.2 = (f32[32,4,1]{2,1,0:T(4,128)S(1)}, f32[32,4,1]{2,1,0:T(4,128)S(1)}, u32[]{:S(2)}, u32[]{:S(2)}) collective-permute-start(f32[32,4,1]{2,1,0:T(4,128)S(1)} %get-tuple-element.114), channel_id=1, source_target_pairs={{0,2},{2,4},{4,6},{6,8},{8,10},{10,12},{12,14},{14,16},{16,18},{18... | collective-permute-start | bytes 1544 | tf_op jit(solution)/shard_map/ppermute | solution.py:21
  59.9 5.2 %collective-permute-start.3 = (f32[32,4,1]{2,1,0:T(4,128)S(1)}, f32[32,4,1]{2,1,0:T(4,128)S(1)}, u32[]{:S(2)}, u32[]{:S(2)}) collective-permute-start(f32[32,4,1]{2,1,0:T(4,128)S(1)} %get-tuple-element.115), channel_id=1, source_target_pairs={{2,0},{4,2},{6,4},{8,6},{10,8},{12,10},{14,12},{16,14},{18,16},{20... | collective-permute-start | bytes 1544 | tf_op jit(solution)/shard_map/ppermute | solution.py:23
  67.4 4.3 %collective-permute-start.4 = (f32[32,4,1]{2,1,0:T(4,128)S(1)}, f32[32,4,1]{2,1,0:T(4,128)S(1)}, u32[]{:S(2)}, u32[]{:S(2)}) collective-permute-start(f32[32,4,1]{2,1,0:T(4,128)S(1)} %get-tuple-element.112), channel_id=1, source_target_pairs={{0,2},{2,4},{4,6},{6,8},{8,10},{10,12},{12,14},{14,16},{16,18},{18... | collective-permute-start | bytes 1544 | tf_op jit(solution)/shard_map/ppermute | solution.py:21
  70.3 5.0 %collective-permute-start.5 = (f32[32,4,1]{2,1,0:T(4,128)S(1)}, f32[32,4,1]{2,1,0:T(4,128)S(1)}, u32[]{:S(2)}, u32[]{:S(2)}) collective-permute-start(f32[32,4,1]{2,1,0:T(4,128)S(1)} %get-tuple-element.113), channel_id=1, source_target_pairs={{2,0},{4,2},{6,4},{8,6},{10,8},{12,10},{14,12},{16,14},{18,16},{20... | collective-permute-start | bytes 1544 | tf_op jit(solution)/shard_map/ppermute | solution.py:23
  77.6 6.1 %collective-permute-start.6 = (f32[32,4,1]{2,1,0:T(4,128)S(1)}, f32[32,4,1]{2,1,0:T(4,128)S(1)}, u32[]{:S(2)}, u32[]{:S(2)}) collective-permute-start(f32[32,4,1]{2,1,0:T(4,128)S(1)} %get-tuple-element.110), channel_id=1, source_target_pairs={{0,2},{2,4},{4,6},{6,8},{8,10},{10,12},{12,14},{14,16},{16,18},{18... | collective-permute-start | bytes 1544 | tf_op jit(solution)/shard_map/ppermute | solution.py:21
  82.2 5.0 %collective-permute-start.7 = (f32[32,4,1]{2,1,0:T(4,128)S(1)}, f32[32,4,1]{2,1,0:T(4,128)S(1)}, u32[]{:S(2)}, u32[]{:S(2)}) collective-permute-start(f32[32,4,1]{2,1,0:T(4,128)S(1)} %get-tuple-element.111), channel_id=1, source_target_pairs={{2,0},{4,2},{6,4},{8,6},{10,8},{12,10},{14,12},{16,14},{18,16},{20... | collective-permute-start | bytes 1544 | tf_op jit(solution)/shard_map/ppermute | solution.py:23
  100.6 40.1 %copy-start.4 = (f32[256]{0:T(256)S(1)}, f32[256]{0:T(256)}, u32[]{:S(2)}) copy-start(f32[256]{0:T(256)} %param.18) | copy-start | bytes 3076
  100.7 40.0 %copy-start.9 = (f32[256]{0:T(256)S(1)}, f32[256]{0:T(256)}, u32[]{:S(2)}) copy-start(f32[256]{0:T(256)} %param.17) | copy-start | bytes 3076
  101.8 27.4 %all-to-all-start.1 = ((f32[64,1,1024]{2,1,0:T(1,128)}), f32[64,1,1024]{2,1,0:T(1,128)S(1)}, u32[]{:S(2)}, u32[]{:S(2)}) async-start(f32[64,1,1024]{2,1,0:T(1,128)} %reshape.303), calls=%async_computation.1 | async-start | bytes 524288 | tf_op jit(solution)/shard_map/all_to_all | solution.py:115
  119.7 82.1 %all-gather.4.cloned.1.call-start = ((), (), s32[]{:S(2)}) async-start(), calls=%async_computation.4 | async-start | bytes 2396160 | tf_op jit(solution)/shard_map/all_gather | solution.py:123
  131.3 72.4 %copy-start.10 = (f32[65]{0:T(128)S(1)}, f32[65]{0:T(128)}, u32[]{:S(2)}) copy-start(f32[65]{0:T(128)} %constant.99.clone.1) | copy-start | bytes 784
  140.7 184.7 %copy-start.5 = (f32[256]{0:T(256)}, f32[256]{0:T(256)S(1)}, u32[]{:S(2)}) copy-start(f32[256]{0:T(256)S(1)} %get-tuple-element.121) | copy-start | bytes 3076
  141.6 200.2 %reduce-scatter.2.cloned.1.call-start = ((), (), s32[]{:S(2)}) async-start(), calls=%async_computation.3 | async-start | bytes 1572864 | tf_op jit(solution)/shard_map/reduce_scatter | solution.py:132
Sparse Core Ops, SparseCore 0:
  141.7 60.0 all-gather.3
  331.7 10.1 reduce-scatter.1
